TPU v7x, 32 devices: a whole 2x2x4 slice. The times are simulated.
32 devices in a mesh: node: 4 (over z), dom: 8 (over y, x, core).
Axes of the slice: x: 2, y: 2, z: 4, core: 2. Of those that a mesh axis runs over, the one named last changes fastest.
Arguments:
- probes: float32 [32, 16, 16, 128], P(None, 'dom'), may hold values from -24 to 24
- slope: float32 [16, 16, 128], P('dom'), may hold values from 4 to 6
- root: float32 [16, 16, 128], P('dom'), may hold values from 0.3 to 0.7
- damping: float32 [16, 16, 128], P('dom'), may hold values from 0.3 to 1.2
Outputs:
- moments: float32 [2, 2, 32, 16, 16, 128], P(None, None, 'node', 'dom')
- projections: float32 [2, 2, 32, 32], replicated
All inputs are finite; a program needn't handle non-finite values.
Results may differ from a plain program's by a relative error of at most 0.00013.
Values sent between devices are 32-bit elements; how exact they have to be, the bound alone decides.
A program may use at most 64 MiB of HBM per device.

v0:
```python
import math
import jax
import jax.numpy as jnp
from jax import lax
from jax.sharding import PartitionSpec as P

NODE_DEV = 2
SWEEPS = 8
CENTRE = 0.5
RADIUS = 2.0


def grid_step(source, fields, factor_re, factor_im):
    padded = jnp.pad(fields, ((0, 0), (0, 0), (1, 1), (1, 1), (1, 1)))
    total = padded[:, :, 2:, 1:-1, 1:-1] + padded[:, :, :-2, 1:-1, 1:-1]
    total = total + padded[:, :, 1:-1, 2:, 1:-1] + padded[:, :, 1:-1, :-2, 1:-1]
    total = total + padded[:, :, 1:-1, 1:-1, 2:] + padded[:, :, 1:-1, 1:-1, :-2]
    real_part = source + total[:, 0]
    imag_part = total[:, 1]
    return jnp.stack(
        [
            real_part * factor_re - imag_part * factor_im,
            real_part * factor_im + imag_part * factor_re,
        ],
        axis=1,
    )


def inverse_diagonal(shift_real, shift_imaginary, slope, root, damping, guard):
    zr_col = shift_real[:, None, None, None, None]
    zi_col = shift_imaginary[:, None, None, None, None]
    decay = jnp.exp(-zr_col)
    real_d = slope * (zr_col - root) + damping * (decay * jnp.cos(zi_col))
    imag_d = slope * zi_col - damping * (decay * jnp.sin(zi_col))
    scale = 1.0 / (real_d * real_d + imag_d * imag_d + guard)
    return (real_d * scale, -imag_d * scale)


def per_system(fields, weight_re, weight_im):
    a_col = weight_re[:, None, None, None]
    b_col = weight_im[:, None, None, None]
    return jnp.stack(
        [a_col * fields[:, 0] - b_col * fields[:, 1], a_col * fields[:, 1] + b_col * fields[:, 0]]
    )


def body(probes, slope, root, damping):
    vectors = probes.shape[0]
    planes = probes.shape[1]
    groups = lax.axis_size("node")
    total = NODE_DEV * groups
    first = (lax.axis_index("node") * NODE_DEV).astype(jnp.float32)
    dom_size = lax.axis_size("dom")
    count = NODE_DEV * vectors // dom_size
    replicated = jnp.broadcast_to(probes[None], (NODE_DEV,) + probes.shape).reshape(
        (NODE_DEV * vectors,) + probes.shape[1:]
    )
    own = lax.all_to_all(replicated, "dom", split_axis=0, concat_axis=1, tiled=True)
    slope_all, root_all, damping_all = (
        lax.all_gather(slope, "dom", axis=0, tiled=True),
        lax.all_gather(root, "dom", axis=0, tiled=True),
        lax.all_gather(damping, "dom", axis=0, tiled=True),
    )
    system = lax.axis_index("dom") * count + jnp.arange(count)
    position = first + (system // vectors).astype(jnp.float32)
    theta = 2.0 * math.pi * (position + 0.5) / total
    shift_real = CENTRE + RADIUS * jnp.cos(theta)
    shift_imaginary = RADIUS * jnp.sin(theta)
    qre, qim = inverse_diagonal(
        shift_real, shift_imaginary, slope_all[None], root_all[None], damping_all[None], 0.0
    )
    qre = qre[:, 0]
    qim = qim[:, 0]
    fields = jnp.stack([own * qre, own * qim], axis=1)
    for sweep in range(SWEEPS):
        fields = grid_step(own, fields, qre, qim)
    weight_re = RADIUS * jnp.cos(theta) / total
    weight_im = RADIUS * jnp.sin(theta) / total
    shifted_re = weight_re * shift_real - weight_im * shift_imaginary
    shifted_im = weight_re * shift_imaginary + weight_im * shift_real
    terms = jnp.stack(
        [per_system(fields, weight_re, weight_im), per_system(fields, shifted_re, shifted_im)]
    )
    back = lax.all_to_all(terms, "dom", split_axis=3, concat_axis=2, tiled=True)
    local = jnp.sum(back.reshape((2, 2, NODE_DEV, vectors) + probes.shape[1:]), axis=2)
    flat = local.reshape(4 * vectors, -1)
    basis = probes.reshape(vectors, -1)
    partial_value = lax.dot_general(
        flat,
        basis,
        (((1,), (1,)), ((), ())),
        precision=lax.Precision.HIGHEST,
        preferred_element_type=jnp.float32,
    )
    cells = planes * probes.shape[2] * probes.shape[3] * lax.axis_size("dom")
    projections = lax.psum(partial_value.reshape(2, 2, vectors, vectors) / cells, ("node", "dom"))
    summed = lax.psum(local, "node")
    share = vectors // groups
    moments = lax.dynamic_slice_in_dim(summed, lax.axis_index("node") * share, share, 2)
    return (moments, projections)


def solution(mesh):
    in_specs = (
        P(None, "dom", None, None),
        P("dom", None, None),
        P("dom", None, None),
        P("dom", None, None),
    )
    out_specs = (P(None, None, "node", "dom", None, None), P())
    return jax.shard_map(body, mesh=mesh, in_specs=in_specs, out_specs=out_specs, check_vma=False)
```

profile of v0, /device:TPU:0, one launch (start us, length us, event | category | flops | bytes accessed | tf_op | source)
XLA Modules:
  0.0 260.8 jit_solution(6893673430703613702)
XLA Ops:
  7.2 2.2 broadcast_in_dim.2
  9.4 5.2 %all-to-all-start = ((f32[64,2,16,128]{3,2,1,0:T(8,128)}), f32[64,2,16,128]{3,2,1,0:T(8,128)S(1)}, u32[]{:S(2)}, u32[]{:S(2)}) async-start(f32[64,2,16,128]{3,2,1,0:T(8,128)} %bitcast), calls=%async_computation | async-start | bytes 2097152 | tf_op jit(solution)/shard_map/all_to_all | solution.py:58
  14.6 18.8 %all_gather.9 = f32[16,16,128]{2,1,0:T(8,128)S(1)} all-gather(f32[2,16,128]{2,1,0:T(8,128)S(1)} %copy-done.2), channel_id=1, replica_groups=mesh['node'=4,'dom'=8] {'dom'}, dimensions={0}, use_global_device_ids=true | all-gather | bytes 147456 | tf_op jit(solution)/shard_map/all_gather | solution.py:60
  33.4 8.3 %all_gather.10 = f32[16,16,128]{2,1,0:T(8,128)S(1)} all-gather(f32[2,16,128]{2,1,0:T(8,128)S(1)} %copy-done.3), channel_id=1, replica_groups=mesh['node'=4,'dom'=8] {'dom'}, dimensions={0}, use_global_device_ids=true | all-gather | bytes 147456 | tf_op jit(solution)/shard_map/all_gather | solution.py:61
  41.7 9.1 %all_gather.11 = f32[16,16,128]{2,1,0:T(8,128)S(1)} all-gather(f32[2,16,128]{2,1,0:T(8,128)S(1)} %copy-done.4), channel_id=1, replica_groups=mesh['node'=4,'dom'=8] {'dom'}, dimensions={0}, use_global_device_ids=true | all-gather | bytes 147456 | tf_op jit(solution)/shard_map/all_gather | solution.py:62
  50.8 0.1 multiply_subtract_fusion.12
  50.9 0.0 all-to-all-done
  50.9 0.1 copy.15
  51.0 0.6 fusion.19
  51.6 2.6 select_maximum_fusion.7
  54.2 3.3 %slice_add_fusion.35 = f32[8,2,16,16,128]{4,3,2,0,1:T(8,128)S(1)} fusion(f32[8,2,18,18,130]{4,3,2,0,1:T(8,128)S(1)} %select_maximum_fusion.7), kind=kLoop, calls=%fused_computation.56 | loop fusion | flops 2621440 | bytes 14680064 | tf_op jit(solution)/shard_map/add | solution.py:17
  57.5 0.8 multiply_subtract_fusion.10
  58.3 2.4 select_maximum_fusion.6
  60.7 3.3 %slice_add_fusion.30 = f32[8,2,16,16,128]{4,3,2,0,1:T(8,128)S(1)} fusion(f32[8,2,18,18,130]{4,3,2,0,1:T(8,128)S(1)} %select_maximum_fusion.6), kind=kLoop, calls=%fused_computation.51 | loop fusion | flops 2621440 | bytes 14680064 | tf_op jit(solution)/shard_map/add | solution.py:17
  63.9 0.8 multiply_subtract_fusion.9
  64.7 2.4 select_maximum_fusion.5
  67.1 3.3 %slice_add_fusion.25 = f32[8,2,16,16,128]{4,3,2,0,1:T(8,128)S(1)} fusion(f32[8,2,18,18,130]{4,3,2,0,1:T(8,128)S(1)} %select_maximum_fusion.5), kind=kLoop, calls=%fused_computation.46 | loop fusion | flops 2621440 | bytes 14680064 | tf_op jit(solution)/shard_map/add | solution.py:17
  70.4 0.8 multiply_subtract_fusion.8
  71.2 2.4 select_maximum_fusion.4
  73.6 3.3 %slice_add_fusion.20 = f32[8,2,16,16,128]{4,3,2,0,1:T(8,128)S(1)} fusion(f32[8,2,18,18,130]{4,3,2,0,1:T(8,128)S(1)} %select_maximum_fusion.4), kind=kLoop, calls=%fused_computation.41 | loop fusion | flops 2621440 | bytes 14680064 | tf_op jit(solution)/shard_map/add | solution.py:17
  76.8 0.8 multiply_subtract_fusion.7
  77.6 2.6 select_maximum_fusion.3
  80.2 3.3 %slice_add_fusion.15 = f32[8,2,16,16,128]{4,3,2,0,1:T(8,128)S(1)} fusion(f32[8,2,18,18,130]{4,3,2,0,1:T(8,128)S(1)} %select_maximum_fusion.3), kind=kLoop, calls=%fused_computation.36 | loop fusion | flops 2621440 | bytes 14680064 | tf_op jit(solution)/shard_map/add | solution.py:17
  83.5 0.8 multiply_subtract_fusion.6
  84.3 2.4 select_maximum_fusion.2
  86.7 3.3 %slice_add_fusion.10 = f32[8,2,16,16,128]{4,3,2,0,1:T(8,128)S(1)} fusion(f32[8,2,18,18,130]{4,3,2,0,1:T(8,128)S(1)} %select_maximum_fusion.2), kind=kLoop, calls=%fused_computation.31 | loop fusion | flops 2621440 | bytes 14680064 | tf_op jit(solution)/shard_map/add | solution.py:17
  90.0 0.8 multiply_subtract_fusion.5
  90.8 2.4 select_maximum_fusion.1
  93.1 3.3 %slice_add_fusion.5 = f32[8,2,16,16,128]{4,3,2,0,1:T(8,128)S(1)} fusion(f32[8,2,18,18,130]{4,3,2,0,1:T(8,128)S(1)} %select_maximum_fusion.1), kind=kLoop, calls=%fused_computation.26 | loop fusion | flops 2621440 | bytes 14680064 | tf_op jit(solution)/shard_map/add | solution.py:17
  96.4 0.8 multiply_subtract_fusion.4
  97.2 2.4 select_maximum_fusion
  99.6 3.5 %slice_add_fusion = f32[8,2,16,16,128]{4,3,2,0,1:T(8,128)S(1)} fusion(f32[8,2,18,18,130]{4,3,2,0,1:T(8,128)S(1)} %select_maximum_fusion), kind=kLoop, calls=%fused_computation.21 | loop fusion | flops 2621440 | bytes 14680064 | tf_op jit(solution)/shard_map/add | solution.py:17
  103.1 0.9 multiply_subtract_fusion.1
  104.1 0.5 multiply_subtract_fusion
  104.6 0.4 maximum_bitcast_fusion
  105.0 0.4 pad_maximum_fusion
  105.4 0.6 copy.17
  106.0 51.6 %all_to_all.36 = f32[2,2,8,16,16,128]{5,4,2,1,0,3:T(8,128)S(1)} all-to-all(f32[2,2,8,16,16,128]{5,4,2,1,0,3:T(8,128)S(1)} %copy.17), channel_id=1, replica_groups=mesh['node'=4,'dom'=8] {'dom'}, dimensions={3} | all-to-all | bytes 8388608 | tf_op jit(solution)/shard_map/all_to_all | solution.py:84
  157.6 0.5 copy.19
  158.2 0.0 copy-start.1
  158.2 0.5 bitcast_reduce_fusion
  158.7 0.5 copy-done.1
  159.2 3.1 %fusion.10 = f32[2,2,32,32]{3,2,1,0:T(8,128)S(1)} fusion(f32[2,2,32,2,16,128]{5,4,3,2,1,0:T(8,128)S(1)} %bitcast_reduce_fusion, f32[32,2,16,128,1,1]{3,2,1,0,5,4:T(8,128)S(1)} %bitcast.53), kind=kOutput, calls=%fused_computation.66 | convolution fusion | flops 201330688 | bytes 2637824 | tf_op jit(solution)/shard_map/dot_general | solution.py:88
  162.3 0.0 all-reduce.10.cloned.1.call-start
  162.4 0.7 all-reduce.10.cloned.1.call-update
  163.1 42.9 %psum.15 = f32[2,2,32,32]{3,2,1,0:T(8,128)} all-reduce(f32[2,2,32,32]{3,2,1,0:T(8,128)S(1)} %fusion.10), channel_id=1, replica_groups=mesh['node'=4,'dom'=8] {'node','dom'}, use_global_device_ids=true, to_apply=%region_2.3 | all-reduce | flops 4096 | bytes 32768 | tf_op jit(solution)/shard_map/psum | solution.py:96
  206.0 46.1 %all-reduce.10.cloned.1.call-done = f32[2,2,32,2,16,128]{5,4,3,2,1,0:T(8,128)} async-done(((f32[2,2,32,2,16,128]{5,4,3,2,1,0:T(8,128)}), f32[2,2,32,2,16,128]{5,4,3,2,1,0:T(8,128)}) %all-reduce.10.cloned.1.call-update) | async-done | bytes 2097168 | tf_op jit(solution)/shard_map/psum | solution.py:97
  252.1 1.9 constant_dynamic-slice_fusion
  (9 shorter events, 0.1 us)
Async XLA Ops:
  7.2 7.4 %copy-start.2 = (f32[2,16,128]{2,1,0:T(8,128)S(1)}, f32[2,16,128]{2,1,0:T(8,128)}, u32[]{:S(2)}) copy-start(f32[2,16,128]{2,1,0:T(8,128)} %param.5) | copy-start | bytes 49156
  7.2 26.2 %copy-start.3 = (f32[2,16,128]{2,1,0:T(8,128)S(1)}, f32[2,16,128]{2,1,0:T(8,128)}, u32[]{:S(2)}) copy-start(f32[2,16,128]{2,1,0:T(8,128)} %param.6) | copy-start | bytes 49156
  7.2 34.5 %copy-start.4 = (f32[2,16,128]{2,1,0:T(8,128)S(1)}, f32[2,16,128]{2,1,0:T(8,128)}, u32[]{:S(2)}) copy-start(f32[2,16,128]{2,1,0:T(8,128)} %param.7) | copy-start | bytes 49156
  9.4 41.5 %all-to-all-start = ((f32[64,2,16,128]{3,2,1,0:T(8,128)}), f32[64,2,16,128]{3,2,1,0:T(8,128)S(1)}, u32[]{:S(2)}, u32[]{:S(2)}) async-start(f32[64,2,16,128]{3,2,1,0:T(8,128)} %bitcast), calls=%async_computation | async-start | bytes 2097152 | tf_op jit(solution)/shard_map/all_to_all | solution.py:58
  158.2 1.0 copy-start.1
  158.7 3.6 %copy-start = (f32[2,2,32,2,16,128]{5,4,3,2,1,0:T(8,128)}, f32[2,2,32,2,16,128]{5,4,3,2,1,0:T(8,128)S(1)}, u32[]{:S(2)}) copy-start(f32[2,2,32,2,16,128]{5,4,3,2,1,0:T(8,128)S(1)} %bitcast_reduce_fusion) | copy-start | bytes 6291460
  162.3 89.8 %all-reduce.10.cloned.1.call-start = ((), (), s32[]{:S(2)}) async-start(), calls=%async_computation.2 | async-start | bytes 4194304 | tf_op jit(solution)/shard_map/psum | solution.py:97
Sparse Core Ops, SparseCore 0:
  165.5 86.5 all-reduce.9
where the time goes:
time: 261 us
  blocking collectives  131 us (50%)
  other arithmetic  54.8 us (21%)
  waiting for transfers between devices  46.8 us (18%)
  between operations  14.3 us (5%)
  local copies, waits for them, and re-layouts  5.8 us (2%)
  starting transfers between devices  5.24 us (2%)
  matrix products  3.08 us (1%)
    all_to_all x1, blocking collectives, body(): back = lax.all_to_all(terms, 'dom', split_axis=3, concat_axis=2, tiled=True)  51.6 us
    psum x1, waiting for transfers between devices, body(): summed = lax.psum(local, 'node')  46.1 us
    psum x1, blocking collectives, body(): lax.psum(partial_value.reshape(2, 2, vectors, vectors) / cells, ('node',...  42.9 us
    add x8, other arithmetic, grid_step(): total = total + padded[:, :, 1:-1, 1:-1, 2:] + padded[:, :, 1:-1, 1:-1, :-2]  26.4 us
    all_gather x1, blocking collectives, body(): lax.all_gather(slope, 'dom', axis=0, tiled=True)  18.8 us
    another operation x7, other arithmetic, grid_step(): jnp.stack([real_part * factor_re - imag_part * factor_im, real_part * fac...  16.9 us
    all_gather x1, blocking collectives, body(): lax.all_gather(damping, 'dom', axis=0, tiled=True)  9.1 us
    all_gather x1, blocking collectives, body(): lax.all_gather(root, 'dom', axis=0, tiled=True)  8.31 us
  transfers between devices with their start and end apart: 2, of which 1 were waited for; matrix products, arithmetic and copies ran while one was open for 0% of the time, Pallas kernels for 0%

commit v1 on v0

--- a/solution.py
+++ b/solution.py
@@ -93,7 +93,9 @@
         preferred_element_type=jnp.float32,
     )
     cells = planes * probes.shape[2] * probes.shape[3] * lax.axis_size("dom")
-    projections = lax.psum(partial_value.reshape(2, 2, vectors, vectors) / cells, ("node", "dom"))
+    projections = jax.lax.psum(
+        jax.lax.psum(partial_value.reshape(2, 2, vectors, vectors) / cells, "dom"), "node"
+    )
     summed = lax.psum(local, "node")
     share = vectors // groups
     moments = lax.dynamic_slice_in_dim(summed, lax.axis_index("node") * share, share, 2)

time: 261 us -> 263 us (level)
  blocking collectives: 131 us -> 135 us
  waiting for transfers between devices: 46.8 us -> 43.8 us
    psum x1 -> x2, blocking collectives: 42.9 us -> 46.9 us  [the longest x1 23.5 us: body(): jax.lax.psum(partial_value.reshape(2, 2, vectors, vectors) / cells, 'dom')]
    psum x1, waiting for transfers between devices: 46.1 us -> 43.2 us  [body(): summed = lax.psum(local, 'node')]
where the time goes in v1:
time: 263 us; the launch traced here: 262 us
  blocking collectives  135 us (51%)
  other arithmetic  55.1 us (21%)
  waiting for transfers between devices  43.8 us (17%)
  between operations  14.4 us (5%)
  local copies, waits for them, and re-layouts  5.76 us (2%)
  starting transfers between devices  5.24 us (2%)
  matrix products  3.08 us (1%)
    all_to_all x1, blocking collectives, body(): back = lax.all_to_all(terms, 'dom', split_axis=3, concat_axis=2, tiled=True)  51.6 us
    psum x1, waiting for transfers between devices, body(): summed = lax.psum(local, 'node')  43.2 us
    add x8, other arithmetic, grid_step(): total = total + padded[:, :, 1:-1, 1:-1, 2:] + padded[:, :, 1:-1, 1:-1, :-2]  26.4 us
    psum x1, blocking collectives, body(): jax.lax.psum(partial_value.reshape(2, 2, vectors, vectors) / cells, 'dom')  23.5 us
    psum x1, blocking collectives, body(): jax.lax.psum(jax.lax.psum(partial_value.reshape(2, 2, vectors, vectors) /...  23.4 us
    all_gather x1, blocking collectives, body(): lax.all_gather(slope, 'dom', axis=0, tiled=True)  18.8 us
    another operation x7, other arithmetic, grid_step(): jnp.stack([real_part * factor_re - imag_part * factor_im, real_part * fac...  17.1 us
    all_gather x1, blocking collectives, body(): lax.all_gather(damping, 'dom', axis=0, tiled=True)  9.1 us
  transfers between devices with their start and end apart: 2, of which 1 were waited for; matrix products, arithmetic and copies ran while one was open for 0% of the time, Pallas kernels for 0%

profile of v1, /device:TPU:0, one launch (start us, length us, event | category | flops | bytes accessed | tf_op | source)
XLA Modules:
  0.0 262.1 jit_solution(14924875201755681358)
XLA Ops:
  7.2 2.2 broadcast_in_dim.2
  9.4 5.2 %all-to-all-start = ((f32[64,2,16,128]{3,2,1,0:T(8,128)}), f32[64,2,16,128]{3,2,1,0:T(8,128)S(1)}, u32[]{:S(2)}, u32[]{:S(2)}) async-start(f32[64,2,16,128]{3,2,1,0:T(8,128)} %bitcast), calls=%async_computation | async-start | bytes 2097152 | tf_op jit(solution)/shard_map/all_to_all | solution.py:58
  14.6 18.8 %all_gather.9 = f32[16,16,128]{2,1,0:T(8,128)S(1)} all-gather(f32[2,16,128]{2,1,0:T(8,128)S(1)} %copy-done.2), channel_id=1, replica_groups=mesh['node'=4,'dom'=8] {'dom'}, dimensions={0}, use_global_device_ids=true | all-gather | bytes 147456 | tf_op jit(solution)/shard_map/all_gather | solution.py:60
  33.4 8.3 %all_gather.10 = f32[16,16,128]{2,1,0:T(8,128)S(1)} all-gather(f32[2,16,128]{2,1,0:T(8,128)S(1)} %copy-done.3), channel_id=1, replica_groups=mesh['node'=4,'dom'=8] {'dom'}, dimensions={0}, use_global_device_ids=true | all-gather | bytes 147456 | tf_op jit(solution)/shard_map/all_gather | solution.py:61
  41.7 9.1 %all_gather.11 = f32[16,16,128]{2,1,0:T(8,128)S(1)} all-gather(f32[2,16,128]{2,1,0:T(8,128)S(1)} %copy-done.4), channel_id=1, replica_groups=mesh['node'=4,'dom'=8] {'dom'}, dimensions={0}, use_global_device_ids=true | all-gather | bytes 147456 | tf_op jit(solution)/shard_map/all_gather | solution.py:62
  50.8 0.1 multiply_subtract_fusion.12
  50.9 0.1 copy.15
  51.0 0.6 fusion.19
  51.6 2.6 select_maximum_fusion.7
  54.2 3.3 %slice_add_fusion.35 = f32[8,2,16,16,128]{4,3,2,0,1:T(8,128)S(1)} fusion(f32[8,2,18,18,130]{4,3,2,0,1:T(8,128)S(1)} %select_maximum_fusion.7), kind=kLoop, calls=%fused_computation.56 | loop fusion | flops 2621440 | bytes 14680064 | tf_op jit(solution)/shard_map/add | solution.py:17
  57.5 0.8 multiply_subtract_fusion.10
  58.3 2.4 select_maximum_fusion.6
  60.7 3.3 %slice_add_fusion.30 = f32[8,2,16,16,128]{4,3,2,0,1:T(8,128)S(1)} fusion(f32[8,2,18,18,130]{4,3,2,0,1:T(8,128)S(1)} %select_maximum_fusion.6), kind=kLoop, calls=%fused_computation.51 | loop fusion | flops 2621440 | bytes 14680064 | tf_op jit(solution)/shard_map/add | solution.py:17
  64.0 0.8 multiply_subtract_fusion.9
  64.8 2.4 select_maximum_fusion.5
  67.2 3.3 %slice_add_fusion.25 = f32[8,2,16,16,128]{4,3,2,0,1:T(8,128)S(1)} fusion(f32[8,2,18,18,130]{4,3,2,0,1:T(8,128)S(1)} %select_maximum_fusion.5), kind=kLoop, calls=%fused_computation.46 | loop fusion | flops 2621440 | bytes 14680064 | tf_op jit(solution)/shard_map/add | solution.py:17
  70.5 0.8 multiply_subtract_fusion.8
  71.3 2.4 select_maximum_fusion.4
  73.7 3.3 %slice_add_fusion.20 = f32[8,2,16,16,128]{4,3,2,0,1:T(8,128)S(1)} fusion(f32[8,2,18,18,130]{4,3,2,0,1:T(8,128)S(1)} %select_maximum_fusion.4), kind=kLoop, calls=%fused_computation.41 | loop fusion | flops 2621440 | bytes 14680064 | tf_op jit(solution)/shard_map/add | solution.py:17
  77.0 0.8 multiply_subtract_fusion.7
  77.8 2.6 %select_maximum_fusion.3 = f32[8,2,18,18,130]{4,3,2,0,1:T(8,128)S(1)} fusion(f32[8,1,16,16,128]{4,3,2,0,1:T(8,128)S(1)} %get-tuple-element.17, f32[8,1,16,16,128]{4,3,2,0,1:T(8,128)S(1)} %get-tuple-element.16), kind=kLoop, calls=%fused_computation.9 | loop fusion | flops 12130560 | bytes 4792832 | tf_op jit(solution)/shard_map/stack | solution.py:20
  80.4 3.3 %slice_add_fusion.15 = f32[8,2,16,16,128]{4,3,2,0,1:T(8,128)S(1)} fusion(f32[8,2,18,18,130]{4,3,2,0,1:T(8,128)S(1)} %select_maximum_fusion.3), kind=kLoop, calls=%fused_computation.36 | loop fusion | flops 2621440 | bytes 14680064 | tf_op jit(solution)/shard_map/add | solution.py:17
  83.7 0.8 multiply_subtract_fusion.6
  84.5 2.4 select_maximum_fusion.2
  86.9 3.3 %slice_add_fusion.10 = f32[8,2,16,16,128]{4,3,2,0,1:T(8,128)S(1)} fusion(f32[8,2,18,18,130]{4,3,2,0,1:T(8,128)S(1)} %select_maximum_fusion.2), kind=kLoop, calls=%fused_computation.31 | loop fusion | flops 2621440 | bytes 14680064 | tf_op jit(solution)/shard_map/add | solution.py:17
  90.2 0.8 multiply_subtract_fusion.5
  91.0 2.4 select_maximum_fusion.1
  93.4 3.3 %slice_add_fusion.5 = f32[8,2,16,16,128]{4,3,2,0,1:T(8,128)S(1)} fusion(f32[8,2,18,18,130]{4,3,2,0,1:T(8,128)S(1)} %select_maximum_fusion.1), kind=kLoop, calls=%fused_computation.26 | loop fusion | flops 2621440 | bytes 14680064 | tf_op jit(solution)/shard_map/add | solution.py:17
  96.7 0.8 multiply_subtract_fusion.4
  97.4 2.4 select_maximum_fusion
  99.9 3.5 %slice_add_fusion = f32[8,2,16,16,128]{4,3,2,0,1:T(8,128)S(1)} fusion(f32[8,2,18,18,130]{4,3,2,0,1:T(8,128)S(1)} %select_maximum_fusion), kind=kLoop, calls=%fused_computation.21 | loop fusion | flops 2621440 | bytes 14680064 | tf_op jit(solution)/shard_map/add | solution.py:17
  103.4 0.9 multiply_subtract_fusion.1
  104.3 0.5 multiply_subtract_fusion
  104.8 0.4 maximum_bitcast_fusion
  105.2 0.4 pad_maximum_fusion
  105.7 0.6 copy.17
  106.3 51.6 %all_to_all.36 = f32[2,2,8,16,16,128]{5,4,2,1,0,3:T(8,128)S(1)} all-to-all(f32[2,2,8,16,16,128]{5,4,2,1,0,3:T(8,128)S(1)} %copy.17), channel_id=1, replica_groups=mesh['node'=4,'dom'=8] {'dom'}, dimensions={3} | all-to-all | bytes 8388608 | tf_op jit(solution)/shard_map/all_to_all | solution.py:84
  157.9 0.5 copy.19
  158.4 0.0 copy-start.1
  158.4 0.5 bitcast_reduce_fusion
  159.0 0.5 copy-done.1
  159.5 3.1 %fusion.10 = f32[2,2,32,32]{3,2,1,0:T(8,128)S(1)} fusion(f32[2,2,32,2,16,128]{5,4,3,2,1,0:T(8,128)S(1)} %bitcast_reduce_fusion, f32[32,2,16,128,1,1]{3,2,1,0,5,4:T(8,128)S(1)} %bitcast.53), kind=kOutput, calls=%fused_computation.66 | convolution fusion | flops 201330688 | bytes 2637824 | tf_op jit(solution)/shard_map/dot_general | solution.py:88
  162.6 0.0 all-reduce.10.cloned.1.call-start
  162.6 0.7 all-reduce.10.cloned.1.call-update
  163.3 23.5 %psum.22 = f32[2,2,32,32]{3,2,1,0:T(8,128)S(1)} all-reduce(f32[2,2,32,32]{3,2,1,0:T(8,128)S(1)} %fusion.10), channel_id=1, replica_groups=mesh['node'=4,'dom'=8] {'dom'}, use_global_device_ids=true, to_apply=%region_2.3 | all-reduce | flops 4096 | bytes 32768 | tf_op jit(solution)/shard_map/psum | solution.py:97
  186.8 23.4 %psum.23 = f32[2,2,32,32]{3,2,1,0:T(8,128)} all-reduce(f32[2,2,32,32]{3,2,1,0:T(8,128)S(1)} %psum.22), channel_id=1, replica_groups=mesh['node'=4,'dom'=8] {'node'}, use_global_device_ids=true, to_apply=%region_3.4 | all-reduce | flops 4096 | bytes 32768 | tf_op jit(solution)/shard_map/psum | solution.py:96
  210.2 43.2 %all-reduce.10.cloned.1.call-done = f32[2,2,32,2,16,128]{5,4,3,2,1,0:T(8,128)} async-done(((f32[2,2,32,2,16,128]{5,4,3,2,1,0:T(8,128)}), f32[2,2,32,2,16,128]{5,4,3,2,1,0:T(8,128)}) %all-reduce.10.cloned.1.call-update) | async-done | bytes 2097168 | tf_op jit(solution)/shard_map/psum | solution.py:99
  253.4 1.9 constant_dynamic-slice_fusion
  (10 shorter events, 0.1 us)
Async XLA Ops:
  7.2 7.4 %copy-start.2 = (f32[2,16,128]{2,1,0:T(8,128)S(1)}, f32[2,16,128]{2,1,0:T(8,128)}, u32[]{:S(2)}) copy-start(f32[2,16,128]{2,1,0:T(8,128)} %param.5) | copy-start | bytes 49156
  7.2 26.2 %copy-start.3 = (f32[2,16,128]{2,1,0:T(8,128)S(1)}, f32[2,16,128]{2,1,0:T(8,128)}, u32[]{:S(2)}) copy-start(f32[2,16,128]{2,1,0:T(8,128)} %param.6) | copy-start | bytes 49156
  7.2 34.5 %copy-start.4 = (f32[2,16,128]{2,1,0:T(8,128)S(1)}, f32[2,16,128]{2,1,0:T(8,128)}, u32[]{:S(2)}) copy-start(f32[2,16,128]{2,1,0:T(8,128)} %param.7) | copy-start | bytes 49156
  9.4 41.5 %all-to-all-start = ((f32[64,2,16,128]{3,2,1,0:T(8,128)}), f32[64,2,16,128]{3,2,1,0:T(8,128)S(1)}, u32[]{:S(2)}, u32[]{:S(2)}) async-start(f32[64,2,16,128]{3,2,1,0:T(8,128)} %bitcast), calls=%async_computation | async-start | bytes 2097152 | tf_op jit(solution)/shard_map/all_to_all | solution.py:58
  158.4 1.0 copy-start.1
  159.0 3.6 %copy-start = (f32[2,2,32,2,16,128]{5,4,3,2,1,0:T(8,128)}, f32[2,2,32,2,16,128]{5,4,3,2,1,0:T(8,128)S(1)}, u32[]{:S(2)}) copy-start(f32[2,2,32,2,16,128]{5,4,3,2,1,0:T(8,128)S(1)} %bitcast_reduce_fusion) | copy-start | bytes 6291460
  162.6 90.8 %all-reduce.10.cloned.1.call-start = ((), (), s32[]{:S(2)}) async-start(), calls=%async_computation.2 | async-start | bytes 4194304 | tf_op jit(solution)/shard_map/psum | solution.py:99
Sparse Core Ops, SparseCore 0:
  165.7 87.5 all-reduce.9
